TPU v7x, 256 devices: a whole 4x4x8 slice. The times are simulated.
256 devices in a mesh: tm: 32 (over y, x, core), space: 8 (over z).
Axes of the slice: x: 4, y: 4, z: 8, core: 2. Of those that a mesh axis runs over, the one named last changes fastest.
Arguments:
- latent_tokens: bfloat16 [64, 1792, 2240], P('tm', 'space'), may hold values from -6 to 6
- norm_gain: float32 [2240], replicated, may hold values from 0.5 to 1.5
- w_query: bfloat16 [2240, 1120], P('tm', 'space'), may hold values from -0.125 to 0.125
- w_key: bfloat16 [2240, 1120], P('tm', 'space'), may hold values from -0.125 to 0.125
- w_value: bfloat16 [2240, 1120], P('tm', 'space'), may hold values from -0.125 to 0.125
- out_gain: float32 [1120], replicated, may hold values from 0.5 to 1.5
- block_ids: int32 [64], P('tm'), may hold values from 0 to 15, never falling along the last dimension, each value on 1 to 8 neighbouring positions
Outputs:
- attended: bfloat16 [64, 1792, 1120], P('tm', 'space')
Inputs may be any that keep to these rules, and one draw needn't show every extreme that they name: `block_ids`: block numbers never fall from one frame to the next; each of the 16 blocks holds 1 to 8 frames and one holds exactly 8.
All inputs are finite; a program needn't handle non-finite values.
Results may differ from a plain program's by a relative error of at most 0.0065.
Values may be sent and summed in bfloat16 or wider, within the bound.
A program may use at most 192 MiB of HBM per device.

v0:
```python
import jax
import jax.numpy as jnp
from jax import lax
from jax.sharding import PartitionSpec as P

HEAD = 112
HEADS = 10


def gathered(weights):
    columns_full = lax.all_gather(jnp.stack(weights), "space", axis=2, tiled=True)
    return lax.all_gather(columns_full, "tm", axis=1, tiled=True)


def on_device(latent_tokens, norm_gain, w_query, w_key, w_value, out_gain, block_ids):
    frame_count, token_count, width = latent_tokens.shape
    row_count = frame_count * token_count
    values = latent_tokens.reshape(row_count, width).astype(jnp.float32)
    meansq = jnp.mean(values * values, axis=-1, keepdims=True)
    normed = (values * lax.rsqrt(meansq + 1e-06) * norm_gain).astype(jnp.bfloat16)
    pair = gathered((w_key, w_value))
    alone = gathered((w_query,))
    projected = jnp.einsum("rn,cnh->crh", normed, pair, preferred_element_type=jnp.float32)
    channels = projected.shape[2]
    headed = (frame_count, token_count, HEADS, HEAD)
    key = jax.nn.relu(projected[0]).astype(jnp.bfloat16).reshape(headed)
    value = projected[1].astype(jnp.bfloat16).reshape(headed)
    states = jnp.einsum("fthk,fthv->fhkv", key, value, preferred_element_type=jnp.float32)
    states = states.reshape(frame_count, channels, HEAD)
    mine = lax.psum_scatter(states, "space", scatter_dimension=1, tiled=True)
    everyone = lax.all_gather(mine.astype(jnp.bfloat16), "tm", tiled=True)
    all_ids = lax.all_gather(block_ids, "tm", tiled=True)
    reaches = (all_ids[None, :] <= block_ids[:, None]).astype(jnp.bfloat16)
    carried = jnp.einsum("fg,gkv->fkv", reaches, everyone, preferred_element_type=jnp.float32)
    carried = lax.all_gather(carried.astype(jnp.bfloat16), "space", axis=1, tiled=True)
    carried = carried.reshape(frame_count, HEADS, HEAD, HEAD)
    query = jnp.einsum("rn,cnh->crh", normed, alone, preferred_element_type=jnp.float32)[0]
    query = jax.nn.relu(query).astype(jnp.bfloat16).reshape(headed)
    numerator = jnp.einsum("fthk,fhkv->fthv", query, carried, preferred_element_type=jnp.float32)
    head_meansq = jnp.mean(numerator * numerator, axis=-1, keepdims=True)
    result = numerator * lax.rsqrt(head_meansq + 1e-06) * out_gain.reshape(HEADS, HEAD)
    return result.reshape(frame_count, token_count, channels).astype(jnp.bfloat16)


def solution(mesh):
    placed = (
        P("tm", "space", None),
        P(),
        P("tm", "space"),
        P("tm", "space"),
        P("tm", "space"),
        P(),
        P("tm"),
    )
    return jax.shard_map(
        on_device, mesh=mesh, in_specs=placed, out_specs=P("tm", "space", None), check_vma=False
    )
```

profile of v0, /device:TPU:6, one launch (start us, length us, event | category | flops | bytes accessed | tf_op | source)
XLA Modules:
  0.0 274.6 jit_solution(4759564278663120340)
XLA Ops:
  6.5 0.0 copy-start.3
  6.5 0.0 copy-start
  6.5 0.0 all-gather.8.cloned.1.call-start
  6.5 0.9 pad_maximum_fusion
  7.5 0.1 copy.40
  7.6 29.2 %all_gather.22 = bf16[2,70,1120]{1,0,2:T(2,128)(2,1)S(1)} all-gather(bf16[2,70,140]{1,0,2:T(2,128)(2,1)S(1)} %copy.40), channel_id=1, replica_groups=mesh['tm'=32,'space'=8] {'space'}, dimensions={2}, use_global_device_ids=true | all-gather | bytes 352800 | tf_op jit(solution)/shard_map/all_gather | solution.py:11
  36.9 2.2 copy.41
  39.0 0.0 copy-start.7
  39.0 0.0 copy-start.2
  39.0 0.0 all-gather.8.cloned.1.call-update
  39.1 0.0 all-gather.12.cloned.1.call-start
  39.1 0.0 copy-done.3
  39.1 0.1 copy.51
  39.2 25.1 %all-gather.2 = bf16[8,140,70]{2,1,0:T(8,128)(2,1)S(1)} all-gather(bf16[1,140,70]{2,1,0:T(8,128)(2,1)S(1)} %bitcast.50), channel_id=2, replica_groups=mesh['tm'=32,'space'=8] {'space'}, dimensions={0}, use_global_device_ids=true | all-gather | bytes 176400 | tf_op jit(solution)/shard_map/all_gather | solution.py:11
  64.3 0.1 reshape.90
  64.4 0.9 copy.65
  65.3 0.0 all-gather.12.cloned.1.call-update
  65.3 0.0 all-gather.10.cloned.1.call-start
  65.3 0.0 copy-done
  65.3 0.5 multiply_reduce_fusion
  65.8 0.1 rsqrt.21
  65.9 0.0 copy-done.7
  65.9 0.6 dynamic-slice.1
  67.1 0.0 copy-done.2
  67.1 1.8 fusion.3
  68.9 32.0 %all-gather.8.cloned.1.call-done = bf16[2,2240,1120]{2,0,1:T(2,128)(2,1)} async-done(((bf16[2,70,1120]{2,0,1:T(2,128)(2,1)}), bf16[2,2240,1120]{2,0,1:T(2,128)(2,1)}) %all-gather.8.cloned.1.call-update) | async-done | bytes 10035216 | tf_op jit(solution)/shard_map/all_gather | solution.py:12
  100.9 9.5 %fusion.4 = bf16[2,448,1120]{2,1,0:T(8,128)(2,1)S(1)} fusion(bf16[2,2240,1120]{2,0,1:T(2,128)(2,1)} %all-gather.8.cloned.1.call-done, bf16[448,2240]{1,0:T(8,128)(2,1)} %fusion.3), kind=kOutput, calls=%fused_computation.7 | convolution fusion | flops 4495769600 | bytes 14049280 | tf_op jit(solution)/shard_map/rn,cnh->crh/dot_general | solution.py:23
  110.4 1.2 fusion.14
  111.6 4.4 %reshape.88 = bf16[2,224,10,112]{3,2,1,0:T(8,128)(2,1)} reshape(bf16[1,448,1120]{2,1,0:T(8,128)(2,1)} %get-tuple-element.5) | data formatting | bytes 2007040 | tf_op jit(solution)/shard_map/convert_element_type | solution.py:26
  116.0 3.1 %reshape.89 = bf16[2,224,10,112]{3,2,1,0:T(8,128)(2,1)} reshape(bf16[1,448,1120]{2,1,0:T(8,128)(2,1)S(1)} %get-tuple-element.6) | data formatting | bytes 2007040 | tf_op jit(solution)/shard_map/convert_element_type | solution.py:27
  119.1 2.6 fusion.18
  121.8 0.0 copy-start.4
  121.8 0.0 copy-start.6
  121.8 0.0 copy-start.5
  121.8 4.2 %copy.47 = f32[2,1120,112]{2,0,1:T(2,128)S(1)} copy(f32[2,1120,112]{2,1,0:T(8,128)S(1)} %bitcast.46) | data formatting | bytes 2007040 | tf_op jit(solution)/shard_map/reshape | solution.py:29
  126.0 62.4 %all-reduce.3 = bf16[2,1120,112]{2,0,1:T(2,128)(2,1)} all-reduce(f32[2,1120,112]{2,0,1:T(2,128)S(1)} %copy.47), channel_id=4, replica_groups=mesh['tm'=32,'space'=8] {'space'}, use_global_device_ids=true, to_apply=%region_1.2.clone | all-reduce | flops 250880 | bytes 1505280
  188.4 0.9 dynamic-slice_convert_fusion
  189.3 0.6 copy.48
  190.0 0.0 all-gather.10.cloned.1.call-update
  190.0 0.0 copy-done.4
  190.0 0.1 mul.63
  190.1 0.0 copy-done.6
  190.1 0.6 dynamic-slice
  191.2 0.0 copy-done.5
  191.3 0.2 dynamic-update-slice
  191.5 14.1 %all-reduce = s32[64]{0:T(128)S(1)} all-reduce(s32[64]{0:T(128)S(1)} %dynamic-update-slice), channel_id=1, replica_groups=mesh['tm'=32,'space'=8] {'tm'}, use_global_device_ids=true, to_apply=%add | all-reduce | flops 64 | bytes 512
  205.6 1.9 multiply_convert_fusion
  207.5 0.0 copy-start.1
  207.5 0.0 all-gather.12.cloned.1.call-done
  207.5 8.1 %reshape.83 = bf16[2240,1120]{1,0:T(8,128)(2,1)} reshape(bf16[32,70,1120]{2,1,0:T(8,128)(2,1)} %all-gather.12.cloned.1.call-done) | data formatting | bytes 10035200
  215.6 0.0 copy-done.1
  215.6 5.3 %fusion.8 = bf16[1,448,1120]{2,1,0:T(8,128)(2,1)S(1)} fusion(bf16[448,2240]{1,0:T(8,128)(2,1)S(1)} %bitcast.48, bf16[2240,1120]{1,0:T(8,128)(2,1)} %reshape.83), kind=kOutput, calls=%fused_computation.10 | convolution fusion | flops 2248888320 | bytes 8028160 | tf_op jit(solution)/shard_map/rn,cnh->crh/dot_general | solution.py:37
  220.9 2.2 reshape.91
  223.1 13.1 %all-gather.10.cloned.1.call-done = bf16[64,140,112]{2,1,0:T(8,128)(2,1)} async-done(((bf16[2,140,112]{2,1,0:T(8,128)(2,1)}), bf16[64,140,112]{2,1,0:T(8,128)(2,1)}) %all-gather.10.cloned.1.call-update) | async-done | bytes 2007056 | tf_op jit(solution)/shard_map/all_gather | solution.py:31
  236.2 2.2 fusion.21
  238.4 27.0 %all_gather.25 = bf16[2,1120,112]{2,0,1:T(2,128)(2,1)S(1)} all-gather(bf16[2,140,112]{2,0,1:T(2,128)(2,1)S(1)} %fusion.21), channel_id=1, replica_groups=mesh['tm'=32,'space'=8] {'space'}, dimensions={1}, use_global_device_ids=true | all-gather | bytes 564480 | tf_op jit(solution)/shard_map/all_gather | solution.py:35
  265.4 0.9 fusion.9
  266.3 0.4 fusion.11
  266.7 1.4 copy.56
  (3 shorter events, 0.0 us)
Async XLA Ops:
  6.5 32.6 %copy-start.3 = (bf16[70,140]{1,0:T(8,128)(2,1)S(1)}, bf16[70,140]{1,0:T(8,128)(2,1)}, u32[]{:S(2)}) copy-start(bf16[70,140]{1,0:T(8,128)(2,1)} %param.9) | copy-start | bytes 58804
  6.5 58.8 %copy-start = (bf16[2,224,2240]{2,1,0:T(8,128)(2,1)S(1)}, bf16[2,224,2240]{2,1,0:T(8,128)(2,1)}, u32[]{:S(2)}) copy-start(bf16[2,224,2240]{2,1,0:T(8,128)(2,1)} %param.7) | copy-start | bytes 6021124
  6.5 94.4 %all-gather.8.cloned.1.call-start = ((), (), s32[]{:S(2)}) async-start(), calls=%async_computation | async-start | bytes 10644480 | tf_op jit(solution)/shard_map/all_gather | solution.py:12
  39.0 26.9 %copy-start.7 = (u32[256]{0:T(256)S(1)}, u32[256]{0:T(256)}, u32[]{:S(2)}) copy-start(u32[256]{0:T(256)} %constant.27) | copy-start | bytes 3076
  39.0 28.0 %copy-start.2 = (f32[2240]{0:T(1024)S(1)}, f32[2240]{0:T(1024)}, u32[]{:S(2)}) copy-start(f32[2240]{0:T(1024)} %param.8) | copy-start | bytes 26884
  39.1 168.4 %all-gather.12.cloned.1.call-start = ((), (), s32[]{:S(2)}) async-start(), calls=%async_computation.2 | async-start | bytes 5474304 | tf_op jit(solution)/shard_map/all_gather | solution.py:12
  65.3 170.9 %all-gather.10.cloned.1.call-start = ((), (), s32[]{:S(2)}) async-start(), calls=%async_computation.1 | async-start | bytes 2433024 | tf_op jit(solution)/shard_map/all_gather | solution.py:31
  121.8 68.2 %copy-start.4 = (f32[1120]{0:T(1024)S(1)}, f32[1120]{0:T(1024)}, u32[]{:S(2)}) copy-start(f32[1120]{0:T(1024)} %param.12) | copy-start | bytes 13444
  121.8 68.3 %copy-start.6 = (u32[256]{0:T(256)S(1)}, u32[256]{0:T(256)}, u32[]{:S(2)}) copy-start(u32[256]{0:T(256)} %constant.21) | copy-start | bytes 3076
  121.8 69.4 %copy-start.5 = (s32[2]{0:T(128)S(1)}, s32[2]{0:T(128)}, u32[]{:S(2)}) copy-start(s32[2]{0:T(128)} %param.13) | copy-start | bytes 28
  207.5 8.1 %copy-start.1 = (bf16[2,224,2240]{2,1,0:T(8,128)(2,1)S(1)}, bf16[2,224,2240]{2,1,0:T(8,128)(2,1)}, u32[]{:S(2)}) copy-start(bf16[2,224,2240]{2,1,0:T(8,128)(2,1)} %multiply_convert_fusion) | copy-start | bytes 6021124
Sparse Core Ops, SparseCore 0:
  39.2 61.6 all-gather.7
  103.5 51.7 all-gather.11
  190.1 46.0 all-gather.9
where the time goes:
time: 275 us
  blocking collectives  158 us (57%)
  waiting for transfers between devices  45.1 us (16%)
  local copies, waits for them, and re-layouts  29.9 us (11%)
  matrix products  20.5 us (7%)
  between operations  14.4 us (5%)
  other arithmetic  6.73 us (2%)
    unnamed x2, blocking collectives  76.5 us
    all_gather x2, blocking collectives, gathered(): lax.all_gather(jnp.stack(weights), 'space', axis=2, tiled=True)  54.3 us
    all_gather x2, waiting for transfers between devices, gathered(): return lax.all_gather(columns_full, 'tm', axis=1, tiled=True)  32 us
    all_gather x1, blocking collectives, on_device(): lax.all_gather(carried.astype(jnp.bfloat16), 'space', axis=1, tiled=True)  27 us
    all_gather x1, waiting for transfers between devices, on_device(): everyone = lax.all_gather(mine.astype(jnp.bfloat16), 'tm', tiled=True)  13.1 us
    unnamed x24, local copies, waits for them, and re-layouts  10.6 us
    dot_general x1, matrix products, on_device(): jnp.einsum('rn,cnh->crh', normed, pair, preferred_element_type=jnp.float32)  9.52 us
  transfers between devices with their start and end apart: 3, of which 2 were waited for; matrix products, arithmetic and copies ran while one was open for 18% of the time, Pallas kernels for 0%

commit v1 on v0

--- a/solution.py
+++ b/solution.py
@@ -7,8 +7,33 @@
 HEADS = 10
 
 
+def cover_the_rings(x0, axis_key):
+    aux = lax.axis_index(axis_key)
+    main = lax.axis_size(axis_key)
+    b_next, carry_in, vec_out = (main, aux, x0.shape[2])
+    by_place = [(i, (i + 1) % b_next) for i in range(b_next)]
+    z2 = jnp.zeros((*x0.shape[:2], b_next * vec_out, *x0.shape[3:]), x0.dtype)
+    z2 = lax.dynamic_update_slice_in_dim(z2, x0, carry_in * vec_out, axis=2)
+    part_now = response = x0
+    later = b_next // 2
+    dev_i = 1
+    so_far_all = [(i, (i - 1) % b_next) for i in range(b_next)]
+    while dev_i < later + 1:
+        part_now = lax.ppermute(part_now, axis_key, perm=by_place)
+        z2 = lax.dynamic_update_slice_in_dim(
+            z2, part_now, (carry_in - dev_i) % b_next * vec_out, axis=2
+        )
+        if dev_i < b_next - later:
+            response = lax.ppermute(response, axis_name=axis_key, perm=so_far_all)
+            z2 = lax.dynamic_update_slice_in_dim(
+                z2, response, (carry_in + dev_i) % b_next * vec_out, axis=2
+            )
+        dev_i = dev_i + 1
+    return z2
+
+
 def gathered(weights):
-    columns_full = lax.all_gather(jnp.stack(weights), "space", axis=2, tiled=True)
+    columns_full = cover_the_rings(jnp.stack(weights), "space")
     return lax.all_gather(columns_full, "tm", axis=1, tiled=True)
 
 

time: 275 us -> 420 us (1.53)
  local copies, waits for them, and re-layouts: 29.9 us -> 210 us
  blocking collectives: 158 us -> 104 us
  starting transfers between devices: 0.09 us -> 23.7 us
  waiting for transfers between devices: 45.1 us -> 33.2 us
    dynamic_update_slice x0 -> x16, local copies, waits for them, and re-layouts: none -> 189 us  [the longest x8 103 us: cover_the_rings(): lax.dynamic_update_slice_in_dim(z2, part_now, (carry_in - dev_i) % b_next...]
    all_gather x2 -> x0, blocking collectives: 54.3 us -> none  [gathered(): lax.all_gather(jnp.stack(weights), 'space', axis=2, tiled=True)]
    all_gather x2, waiting for transfers between devices: 32 us -> 0.01 us  [gathered(): return lax.all_gather(columns_full, 'tm', axis=1, tiled=True)]
    ppermute x0 -> x14, starting transfers between devices: none -> 23.4 us  [the longest x6 20.8 us: cover_the_rings(): response = lax.ppermute(response, axis_name=axis_key, perm=so_far_all)]
    ppermute x0 -> x14, waiting for transfers between devices: none -> 12.2 us  [the longest x8 12.2 us: cover_the_rings(): part_now = lax.ppermute(part_now, axis_key, perm=by_place)]
    all_gather x1, waiting for transfers between devices: 13.1 us -> 21 us  [on_device(): everyone = lax.all_gather(mine.astype(jnp.bfloat16), 'tm', tiled=True)]
    unnamed x24 -> x22, local copies, waits for them, and re-layouts: 10.6 us -> 3.05 us
  transfers between devices with their start and end apart: 3 -> 17, of which waited for: 2 -> 7; matrix products, arithmetic and copies ran while one was open for 18% -> 53% of each run, Pallas kernels for 0% -> 0%
where the time goes in v1:
time: 420 us; the launch traced here: 416 us
  local copies, waits for them, and re-layouts  210 us (50%)
  blocking collectives  104 us (25%)
  waiting for transfers between devices  33.2 us (8%)
  starting transfers between devices  23.7 us (6%)
  matrix products  22.7 us (5%)
  between operations  15.4 us (4%)
  other arithmetic  6.54 us (2%)
    dynamic_update_slice x8, local copies, waits for them, and re-layouts, cover_the_rings(): lax.dynamic_update_slice_in_dim(z2, part_now, (carry_in - dev_i) % b_next...  103 us
    dynamic_update_slice x6, local copies, waits for them, and re-layouts, cover_the_rings(): lax.dynamic_update_slice_in_dim(z2, response, (carry_in + dev_i) % b_next...  77.8 us
    unnamed x2, blocking collectives  76.9 us
    all_gather x1, blocking collectives, on_device(): lax.all_gather(carried.astype(jnp.bfloat16), 'space', axis=1, tiled=True)  27 us
    all_gather x1, waiting for transfers between devices, on_device(): everyone = lax.all_gather(mine.astype(jnp.bfloat16), 'tm', tiled=True)  21 us
    ppermute x6, starting transfers between devices, cover_the_rings(): response = lax.ppermute(response, axis_name=axis_key, perm=so_far_all)  20.8 us
    ppermute x8, waiting for transfers between devices, cover_the_rings(): part_now = lax.ppermute(part_now, axis_key, perm=by_place)  12.2 us
    dot_general x1, matrix products, on_device(): jnp.einsum('rn,cnh->crh', normed, pair, preferred_element_type=jnp.float32)  9.52 us
  transfers between devices with their start and end apart: 17, of which 7 were waited for; matrix products, arithmetic and copies ran while one was open for 53% of the time, Pallas kernels for 0%

profile of v1, /device:TPU:6, one launch (start us, length us, event | category | flops | bytes accessed | tf_op | source)
XLA Modules:
  0.0 415.9 jit_solution(3817728522846931052)
XLA Ops:
  6.5 0.8 pad_maximum_fusion
  7.4 2.0 collective-permute-start
  9.4 4.0 collective-permute-start.1
  13.4 2.2 collective-permute-done
  15.6 3.3 collective-permute-start.3
  18.9 2.2 collective-permute-done.2
  21.2 3.3 collective-permute-start.5
  24.5 2.2 collective-permute-done.4
  26.8 0.5 collective-permute-start.6
  27.5 0.2 broadcast_in_dim.4
  27.7 4.0 dynamic_update_slice.48
  31.8 12.8 %dynamic_update_slice.49 = bf16[2,70,1120]{2,0,1:T(2,128)(2,1)S(1)} dynamic-update-slice(bf16[2,70,1120]{2,0,1:T(2,128)(2,1)S(1)} %dynamic_update_slice.48, bf16[2,70,140]{2,0,1:T(2,128)(2,1)S(1)} %copy.35, s32[]{:T(128)} %constant.75.clone.1, s32[]{:T(128)} %constant.75.clone.1, s32[]{:T(128)S(6)} %select_n.79) | dynamic-update-slice | bytes 78404 | tf_op jit(solution)/shard_map/dynamic_update_slice | solution.py:23
  44.6 13.0 %dynamic_update_slice.50 = bf16[2,70,1120]{2,0,1:T(2,128)(2,1)S(1)} dynamic-update-slice(bf16[2,70,1120]{2,0,1:T(2,128)(2,1)S(1)} %dynamic_update_slice.49, bf16[2,70,140]{2,0,1:T(2,128)(2,1)S(1)} %copy.36, s32[]{:T(128)} %constant.75.clone.1, s32[]{:T(128)} %constant.75.clone.1, s32[]{:T(128)S(6)} %select_n.81) | dynamic-update-slice | bytes 78404 | tf_op jit(solution)/shard_map/dynamic_update_slice | solution.py:28
  57.6 13.0 %dynamic_update_slice.51 = bf16[2,70,1120]{2,0,1:T(2,128)(2,1)S(1)} dynamic-update-slice(bf16[2,70,1120]{2,0,1:T(2,128)(2,1)S(1)} %dynamic_update_slice.50, bf16[2,70,140]{2,0,1:T(2,128)(2,1)S(1)} %copy.37, s32[]{:T(128)} %constant.75.clone.1, s32[]{:T(128)} %constant.75.clone.1, s32[]{:T(128)S(6)} %select_n.83) | dynamic-update-slice | bytes 78404 | tf_op jit(solution)/shard_map/dynamic_update_slice | solution.py:23
  70.7 13.0 %dynamic_update_slice.52 = bf16[2,70,1120]{2,0,1:T(2,128)(2,1)S(1)} dynamic-update-slice(bf16[2,70,1120]{2,0,1:T(2,128)(2,1)S(1)} %dynamic_update_slice.51, bf16[2,70,140]{2,0,1:T(2,128)(2,1)S(1)} %copy.38, s32[]{:T(128)} %constant.75.clone.1, s32[]{:T(128)} %constant.75.clone.1, s32[]{:T(128)S(6)} %select_n.85) | dynamic-update-slice | bytes 78404 | tf_op jit(solution)/shard_map/dynamic_update_slice | solution.py:28
  83.7 13.0 %dynamic_update_slice.53 = bf16[2,70,1120]{2,0,1:T(2,128)(2,1)S(1)} dynamic-update-slice(bf16[2,70,1120]{2,0,1:T(2,128)(2,1)S(1)} %dynamic_update_slice.52, bf16[2,70,140]{2,0,1:T(2,128)(2,1)S(1)} %copy.39, s32[]{:T(128)} %constant.75.clone.1, s32[]{:T(128)} %constant.75.clone.1, s32[]{:T(128)S(6)} %select_n.87) | dynamic-update-slice | bytes 78404 | tf_op jit(solution)/shard_map/dynamic_update_slice | solution.py:23
  96.7 0.1 copy.40
  96.8 13.0 %dynamic_update_slice.54 = bf16[2,70,1120]{2,0,1:T(2,128)(2,1)S(1)} dynamic-update-slice(bf16[2,70,1120]{2,0,1:T(2,128)(2,1)S(1)} %dynamic_update_slice.53, bf16[2,70,140]{2,0,1:T(2,128)(2,1)S(1)} %copy.40, s32[]{:T(128)} %constant.75.clone.1, s32[]{:T(128)} %constant.75.clone.1, s32[]{:T(128)S(6)} %select_n.89) | dynamic-update-slice | bytes 78404 | tf_op jit(solution)/shard_map/dynamic_update_slice | solution.py:28
  109.8 13.0 %dynamic_update_slice.55 = bf16[2,70,1120]{2,0,1:T(2,128)(2,1)S(1)} dynamic-update-slice(bf16[2,70,1120]{2,0,1:T(2,128)(2,1)S(1)} %dynamic_update_slice.54, bf16[2,70,140]{2,0,1:T(2,128)(2,1)S(1)} %copy.41, s32[]{:T(128)} %constant.75.clone.1, s32[]{:T(128)} %constant.75.clone.1, s32[]{:T(128)S(6)} %select_n.91) | dynamic-update-slice | bytes 78404 | tf_op jit(solution)/shard_map/dynamic_update_slice | solution.py:23
  122.8 0.7 copy-done.2
  123.6 0.1 collective-permute-start.7
  123.7 3.3 collective-permute-start.8
  126.9 2.0 collective-permute-done.7
  128.9 3.4 collective-permute-start.10
  132.4 1.7 collective-permute-done.9
  134.1 3.4 collective-permute-start.12
  137.6 1.7 collective-permute-done.11
  139.3 0.2 broadcast_in_dim.5
  139.5 4.0 dynamic_update_slice.56
  143.7 12.8 %dynamic_update_slice.57 = bf16[1,70,1120]{2,0,1:T(2,128)(2,1)S(1)} dynamic-update-slice(bf16[1,70,1120]{2,0,1:T(2,128)(2,1)S(1)} %dynamic_update_slice.56, bf16[1,70,140]{2,0,1:T(2,128)(2,1)S(1)} %copy.52, s32[]{:T(128)} %constant.75.clone.1, s32[]{:T(128)} %constant.75.clone.1, s32[]{:T(128)S(6)} %select_n.79) | dynamic-update-slice | bytes 39204 | tf_op jit(solution)/shard_map/dynamic_update_slice | solution.py:23
  156.5 13.0 %dynamic_update_slice.58 = bf16[1,70,1120]{2,0,1:T(2,128)(2,1)S(1)} dynamic-update-slice(bf16[1,70,1120]{2,0,1:T(2,128)(2,1)S(1)} %dynamic_update_slice.57, bf16[1,70,140]{2,0,1:T(2,128)(2,1)S(1)} %copy.53, s32[]{:T(128)} %constant.75.clone.1, s32[]{:T(128)} %constant.75.clone.1, s32[]{:T(128)S(6)} %select_n.81) | dynamic-update-slice | bytes 39204 | tf_op jit(solution)/shard_map/dynamic_update_slice | solution.py:28
  169.5 13.0 %dynamic_update_slice.59 = bf16[1,70,1120]{2,0,1:T(2,128)(2,1)S(1)} dynamic-update-slice(bf16[1,70,1120]{2,0,1:T(2,128)(2,1)S(1)} %dynamic_update_slice.58, bf16[1,70,140]{2,0,1:T(2,128)(2,1)S(1)} %copy.54, s32[]{:T(128)} %constant.75.clone.1, s32[]{:T(128)} %constant.75.clone.1, s32[]{:T(128)S(6)} %select_n.83) | dynamic-update-slice | bytes 39204 | tf_op jit(solution)/shard_map/dynamic_update_slice | solution.py:23
  182.6 13.0 %dynamic_update_slice.60 = bf16[1,70,1120]{2,0,1:T(2,128)(2,1)S(1)} dynamic-update-slice(bf16[1,70,1120]{2,0,1:T(2,128)(2,1)S(1)} %dynamic_update_slice.59, bf16[1,70,140]{2,0,1:T(2,128)(2,1)S(1)} %copy.55, s32[]{:T(128)} %constant.75.clone.1, s32[]{:T(128)} %constant.75.clone.1, s32[]{:T(128)S(6)} %select_n.85) | dynamic-update-slice | bytes 39204 | tf_op jit(solution)/shard_map/dynamic_update_slice | solution.py:28
  195.6 13.0 %dynamic_update_slice.61 = bf16[1,70,1120]{2,0,1:T(2,128)(2,1)S(1)} dynamic-update-slice(bf16[1,70,1120]{2,0,1:T(2,128)(2,1)S(1)} %dynamic_update_slice.60, bf16[1,70,140]{2,0,1:T(2,128)(2,1)S(1)} %copy.56, s32[]{:T(128)} %constant.75.clone.1, s32[]{:T(128)} %constant.75.clone.1, s32[]{:T(128)S(6)} %select_n.87) | dynamic-update-slice | bytes 39204 | tf_op jit(solution)/shard_map/dynamic_update_slice | solution.py:23
  208.6 13.0 %dynamic_update_slice.62 = bf16[1,70,1120]{2,0,1:T(2,128)(2,1)S(1)} dynamic-update-slice(bf16[1,70,1120]{2,0,1:T(2,128)(2,1)S(1)} %dynamic_update_slice.61, bf16[1,70,140]{2,0,1:T(2,128)(2,1)S(1)} %copy.57, s32[]{:T(128)} %constant.75.clone.1, s32[]{:T(128)} %constant.75.clone.1, s32[]{:T(128)S(6)} %select_n.89) | dynamic-update-slice | bytes 39204 | tf_op jit(solution)/shard_map/dynamic_update_slice | solution.py:28
  221.7 13.0 %dynamic_update_slice.63 = bf16[1,70,1120]{2,0,1:T(2,128)(2,1)S(1)} dynamic-update-slice(bf16[1,70,1120]{2,0,1:T(2,128)(2,1)S(1)} %dynamic_update_slice.62, bf16[1,70,140]{2,0,1:T(2,128)(2,1)S(1)} %copy.58, s32[]{:T(128)} %constant.75.clone.1, s32[]{:T(128)} %constant.75.clone.1, s32[]{:T(128)S(6)} %select_n.91) | dynamic-update-slice | bytes 39204 | tf_op jit(solution)/shard_map/dynamic_update_slice | solution.py:23
  234.7 0.7 copy-done.1
  235.4 0.3 all-gather.6.cloned.1.call-start
  235.7 0.5 multiply_reduce_fusion
  236.2 0.1 rsqrt.21
  236.3 0.7 dynamic-slice.1
  237.6 1.9 fusion.6
  239.5 9.5 %fusion.7 = bf16[2,448,1120]{2,1,0:T(8,128)(2,1)S(1)} fusion(bf16[2,2240,1120]{2,0,1:T(2,128)(2,1)} %all-gather.4.cloned.1.call-done, bf16[448,2240]{1,0:T(8,128)(2,1)} %fusion.6), kind=kOutput, calls=%fused_computation.10 | convolution fusion | flops 4495769600 | bytes 14049280 | tf_op jit(solution)/shard_map/rn,cnh->crh/dot_general | solution.py:48
  249.0 1.2 fusion.24
  250.2 4.5 %reshape.81 = bf16[2,224,10,112]{3,2,1,0:T(8,128)(2,1)} reshape(bf16[1,448,1120]{2,1,0:T(8,128)(2,1)} %get-tuple-element.5) | data formatting | bytes 2007040 | tf_op jit(solution)/shard_map/convert_element_type | solution.py:51
  254.6 3.1 reshape.82
  257.7 2.7 fusion.28
  260.4 4.2 %copy.47 = f32[2,1120,112]{2,0,1:T(2,128)S(1)} copy(f32[2,1120,112]{2,1,0:T(8,128)S(1)} %bitcast.47) | data formatting | bytes 2007040 | tf_op jit(solution)/shard_map/reshape | solution.py:54
  264.6 61.9 %all-reduce.3 = bf16[2,1120,112]{2,0,1:T(2,128)(2,1)} all-reduce(f32[2,1120,112]{2,0,1:T(2,128)S(1)} %copy.47), channel_id=2, replica_groups=mesh['tm'=32,'space'=8] {'space'}, use_global_device_ids=true, to_apply=%region_1.2.clone | all-reduce | flops 250880 | bytes 1505280
  326.5 0.9 dynamic-slice_convert_fusion
  327.4 0.6 copy.48
  328.1 0.1 mul.103
  328.2 0.7 dynamic-slice
  329.5 0.2 dynamic-update-slice
  329.8 15.0 %all-reduce = s32[64]{0:T(128)S(1)} all-reduce(s32[64]{0:T(128)S(1)} %dynamic-update-slice), channel_id=1, replica_groups=mesh['tm'=32,'space'=8] {'tm'}, use_global_device_ids=true, to_apply=%add | all-reduce | flops 64 | bytes 512
  344.8 1.8 multiply_convert_fusion
  346.6 7.4 %fusion.16 = bf16[1,448,1120]{2,1,0:T(8,128)(2,1)S(1)} fusion(bf16[448,2240]{1,0:T(8,128)(2,1)} %bitcast.49, bf16[1,2240,1120]{2,0,1:T(2,128)(2,1)} %all-gather.8.cloned.1.call-done), kind=kOutput, calls=%fused_computation.13 | convolution fusion | flops 2248888320 | bytes 8028160 | tf_op jit(solution)/shard_map/rn,cnh->crh/dot_general | solution.py:62
  354.0 2.2 reshape.83
  356.2 21.0 %all-gather.6.cloned.1.call-done = bf16[64,140,112]{2,1,0:T(8,128)(2,1)} async-done(((bf16[2,140,112]{2,1,0:T(8,128)(2,1)}), bf16[64,140,112]{2,1,0:T(8,128)(2,1)}) %all-gather.6.cloned.1.call-update) | async-done | bytes 2007056 | tf_op jit(solution)/shard_map/all_gather | solution.py:56
  377.2 2.2 fusion.31
  379.4 27.0 %all_gather.18 = bf16[2,1120,112]{2,0,1:T(2,128)(2,1)S(1)} all-gather(bf16[2,140,112]{2,0,1:T(2,128)(2,1)S(1)} %fusion.31), channel_id=1, replica_groups=mesh['tm'=32,'space'=8] {'space'}, dimensions={1}, use_global_device_ids=true | all-gather | bytes 564480 | tf_op jit(solution)/shard_map/all_gather | solution.py:60
  406.4 0.9 fusion.19
  407.4 0.4 fusion.21
  407.7 1.4 copy.62
  (54 shorter events, 1.1 us)
Async XLA Ops:
  6.5 117.0 %copy-start.4 = (bf16[70,140]{1,0:T(8,128)(2,1)S(1)}, bf16[70,140]{1,0:T(8,128)(2,1)}, u32[]{:S(2)}) copy-start(bf16[70,140]{1,0:T(8,128)(2,1)} %param.9) | copy-start | bytes 58804
  6.5 232.9 %all-gather.4.cloned.1.call-start = ((), (), s32[]{:S(2)}) async-start(), calls=%async_computation | async-start | bytes 10644480 | tf_op jit(solution)/shard_map/all_gather | solution.py:37
  7.4 8.3 %collective-permute-start = (bf16[2,70,140]{2,1,0:T(8,128)(2,1)S(1)}, bf16[2,70,140]{2,1,0:T(8,128)(2,1)S(1)}, u32[]{:S(2)}, u32[]{:S(2)}) collective-permute-start(bf16[2,70,140]{2,1,0:T(8,128)(2,1)S(1)} %pad_maximum_fusion), channel_id=1, source_target_pairs={{0,1},{1,2},{2,3},{3,4},{4,5},{5,6},{6,7},{7,0},{8,9},{9,10},{10,1... | collective-permute-start | bytes 117608 | tf_op jit(solution)/shard_map/ppermute | solution.py:22
  9.4 6.3 %collective-permute-start.1 = (bf16[2,70,140]{2,1,0:T(8,128)(2,1)S(1)}, bf16[2,70,140]{2,1,0:T(8,128)(2,1)S(1)}, u32[]{:S(2)}, u32[]{:S(2)}) collective-permute-start(bf16[2,70,140]{2,1,0:T(8,128)(2,1)S(1)} %pad_maximum_fusion), channel_id=1, source_target_pairs={{0,7},{1,0},{2,1},{3,2},{4,3},{5,4},{6,5},{7,6},{8,15},{9,8},{10,9... | collective-permute-start | bytes 117608 | tf_op jit(solution)/shard_map/ppermute | solution.py:27
  15.6 5.6 %collective-permute-start.2 = (bf16[2,70,140]{2,1,0:T(8,128)(2,1)S(1)}, bf16[2,70,140]{2,1,0:T(8,128)(2,1)S(1)}, u32[]{:S(2)}, u32[]{:S(2)}) collective-permute-start(bf16[2,70,140]{2,1,0:T(8,128)(2,1)S(1)} %collective-permute-done), channel_id=1, source_target_pairs={{0,1},{1,2},{2,3},{3,4},{4,5},{5,6},{6,7},{7,0},{8,9},{9,10},{10,1... | collective-permute-start | bytes 117608 | tf_op jit(solution)/shard_map/ppermute | solution.py:22
  15.6 5.6 %collective-permute-start.3 = (bf16[2,70,140]{2,1,0:T(8,128)(2,1)S(1)}, bf16[2,70,140]{2,1,0:T(8,128)(2,1)S(1)}, u32[]{:S(2)}, u32[]{:S(2)}) collective-permute-start(bf16[2,70,140]{2,1,0:T(8,128)(2,1)S(1)} %collective-permute-done.1), channel_id=1, source_target_pairs={{0,7},{1,0},{2,1},{3,2},{4,3},{5,4},{6,5},{7,6},{8,15},{9,8},{10,9... | collective-permute-start | bytes 117608 | tf_op jit(solution)/shard_map/ppermute | solution.py:27
  21.2 5.6 %collective-permute-start.4 = (bf16[2,70,140]{2,1,0:T(8,128)(2,1)S(1)}, bf16[2,70,140]{2,1,0:T(8,128)(2,1)S(1)}, u32[]{:S(2)}, u32[]{:S(2)}) collective-permute-start(bf16[2,70,140]{2,1,0:T(8,128)(2,1)S(1)} %collective-permute-done.2), channel_id=1, source_target_pairs={{0,1},{1,2},{2,3},{3,4},{4,5},{5,6},{6,7},{7,0},{8,9},{9,10},{10,1... | collective-permute-start | bytes 117608 | tf_op jit(solution)/shard_map/ppermute | solution.py:22
  21.2 75.5 %collective-permute-start.5 = (bf16[2,70,140]{2,1,0:T(8,128)(2,1)S(1)}, bf16[2,70,140]{2,1,0:T(8,128)(2,1)S(1)}, u32[]{:S(2)}, u32[]{:S(2)}) collective-permute-start(bf16[2,70,140]{2,1,0:T(8,128)(2,1)S(1)} %collective-permute-done.3), channel_id=1, source_target_pairs={{0,7},{1,0},{2,1},{3,2},{4,3},{5,4},{6,5},{7,6},{8,15},{9,8},{10,9... | collective-permute-start | bytes 117608 | tf_op jit(solution)/shard_map/ppermute | solution.py:27
  26.8 83.0 %collective-permute-start.6 = (bf16[2,70,140]{2,1,0:T(8,128)(2,1)S(1)}, bf16[2,70,140]{2,1,0:T(8,128)(2,1)S(1)}, u32[]{:S(2)}, u32[]{:S(2)}) collective-permute-start(bf16[2,70,140]{2,1,0:T(8,128)(2,1)S(1)} %collective-permute-done.4), channel_id=1, source_target_pairs={{0,1},{1,2},{2,3},{3,4},{4,5},{5,6},{6,7},{7,0},{8,9},{9,10},{10,1... | collective-permute-start | bytes 117608 | tf_op jit(solution)/shard_map/ppermute | solution.py:22
  70.6 165.1 %copy-start = (bf16[2,224,2240]{2,1,0:T(8,128)(2,1)S(1)}, bf16[2,224,2240]{2,1,0:T(8,128)(2,1)}, u32[]{:S(2)}) copy-start(bf16[2,224,2240]{2,1,0:T(8,128)(2,1)} %param.7) | copy-start | bytes 6021124
  122.8 0.7 copy-start.2
  123.5 223.1 %all-gather.8.cloned.1.call-start = ((), (), s32[]{:S(2)}) async-start(), calls=%async_computation.2 | async-start | bytes 10644480 | tf_op jit(solution)/shard_map/all_gather | solution.py:37
  123.6 5.4 %collective-permute-start.7 = (bf16[1,70,140]{2,1,0:T(8,128)(2,1)S(1)}, bf16[1,70,140]{2,1,0:T(8,128)(2,1)S(1)}, u32[]{:S(2)}, u32[]{:S(2)}) collective-permute-start(bf16[1,70,140]{2,1,0:T(8,128)(2,1)S(1)} %bitcast.50), channel_id=1, source_target_pairs={{0,1},{1,2},{2,3},{3,4},{4,5},{5,6},{6,7},{7,0},{8,9},{9,10},{10,1... | collective-permute-start | bytes 58808 | tf_op jit(solution)/shard_map/ppermute | solution.py:22
  123.7 5.3 %collective-permute-start.8 = (bf16[1,70,140]{2,1,0:T(8,128)(2,1)S(1)}, bf16[1,70,140]{2,1,0:T(8,128)(2,1)S(1)}, u32[]{:S(2)}, u32[]{:S(2)}) collective-permute-start(bf16[1,70,140]{2,1,0:T(8,128)(2,1)S(1)} %bitcast.51), channel_id=1, source_target_pairs={{0,7},{1,0},{2,1},{3,2},{4,3},{5,4},{6,5},{7,6},{8,15},{9,8},{10,9... | collective-permute-start | bytes 58808 | tf_op jit(solution)/shard_map/ppermute | solution.py:27
  128.9 5.2 %collective-permute-start.9 = (bf16[1,70,140]{2,1,0:T(8,128)(2,1)S(1)}, bf16[1,70,140]{2,1,0:T(8,128)(2,1)S(1)}, u32[]{:S(2)}, u32[]{:S(2)}) collective-permute-start(bf16[1,70,140]{2,1,0:T(8,128)(2,1)S(1)} %collective-permute-done.7), channel_id=1, source_target_pairs={{0,1},{1,2},{2,3},{3,4},{4,5},{5,6},{6,7},{7,0},{8,9},{9,10},{10,1... | collective-permute-start | bytes 58808 | tf_op jit(solution)/shard_map/ppermute | solution.py:22
  128.9 5.2 %collective-permute-start.10 = (bf16[1,70,140]{2,1,0:T(8,128)(2,1)S(1)}, bf16[1,70,140]{2,1,0:T(8,128)(2,1)S(1)}, u32[]{:S(2)}, u32[]{:S(2)}) collective-permute-start(bf16[1,70,140]{2,1,0:T(8,128)(2,1)S(1)} %collective-permute-done.8), channel_id=1, source_target_pairs={{0,7},{1,0},{2,1},{3,2},{4,3},{5,4},{6,5},{7,6},{8,15},{9,8},{10,9... | collective-permute-start | bytes 58808 | tf_op jit(solution)/shard_map/ppermute | solution.py:27
  134.1 5.2 %collective-permute-start.11 = (bf16[1,70,140]{2,1,0:T(8,128)(2,1)S(1)}, bf16[1,70,140]{2,1,0:T(8,128)(2,1)S(1)}, u32[]{:S(2)}, u32[]{:S(2)}) collective-permute-start(bf16[1,70,140]{2,1,0:T(8,128)(2,1)S(1)} %collective-permute-done.9), channel_id=1, source_target_pairs={{0,1},{1,2},{2,3},{3,4},{4,5},{5,6},{6,7},{7,0},{8,9},{9,10},{10,1... | collective-permute-start | bytes 58808 | tf_op jit(solution)/shard_map/ppermute | solution.py:22
  134.1 74.4 %collective-permute-start.12 = (bf16[1,70,140]{2,1,0:T(8,128)(2,1)S(1)}, bf16[1,70,140]{2,1,0:T(8,128)(2,1)S(1)}, u32[]{:S(2)}, u32[]{:S(2)}) collective-permute-start(bf16[1,70,140]{2,1,0:T(8,128)(2,1)S(1)} %collective-permute-done.10), channel_id=1, source_target_pairs={{0,7},{1,0},{2,1},{3,2},{4,3},{5,4},{6,5},{7,6},{8,15},{9,8},{10,9... | collective-permute-start | bytes 58808 | tf_op jit(solution)/shard_map/ppermute | solution.py:27
  139.3 82.3 %collective-permute-start.13 = (bf16[1,70,140]{2,1,0:T(8,128)(2,1)S(1)}, bf16[1,70,140]{2,1,0:T(8,128)(2,1)S(1)}, u32[]{:S(2)}, u32[]{:S(2)}) collective-permute-start(bf16[1,70,140]{2,1,0:T(8,128)(2,1)S(1)} %collective-permute-done.11), channel_id=1, source_target_pairs={{0,1},{1,2},{2,3},{3,4},{4,5},{5,6},{6,7},{7,0},{8,9},{9,10},{10,1... | collective-permute-start | bytes 58808 | tf_op jit(solution)/shard_map/ppermute | solution.py:22
  143.6 92.6 %copy-start.8 = (u32[256]{0:T(256)S(1)}, u32[256]{0:T(256)}, u32[]{:S(2)}) copy-start(u32[256]{0:T(256)} %constant.105) | copy-start | bytes 3076
  143.7 94.0 %copy-start.3 = (f32[2240]{0:T(1024)S(1)}, f32[2240]{0:T(1024)}, u32[]{:S(2)}) copy-start(f32[2240]{0:T(1024)} %param.8) | copy-start | bytes 26884
  234.6 0.7 copy-start.1
  235.4 141.8 %all-gather.6.cloned.1.call-start = ((), (), s32[]{:S(2)}) async-start(), calls=%async_computation.1 | async-start | bytes 2433024 | tf_op jit(solution)/shard_map/all_gather | solution.py:56
  260.4 67.7 %copy-start.5 = (f32[1120]{0:T(1024)S(1)}, f32[1120]{0:T(1024)}, u32[]{:S(2)}) copy-start(f32[1120]{0:T(1024)} %param.12) | copy-start | bytes 13444
  260.4 67.8 %copy-start.7 = (u32[256]{0:T(256)S(1)}, u32[256]{0:T(256)}, u32[]{:S(2)}) copy-start(u32[256]{0:T(256)} %constant.99) | copy-start | bytes 3076
  260.4 69.1 %copy-start.6 = (s32[2]{0:T(128)S(1)}, s32[2]{0:T(128)}, u32[]{:S(2)}) copy-start(s32[2]{0:T(128)} %param.13) | copy-start | bytes 28
Sparse Core Ops, SparseCore 0:
  123.6 63.6 all-gather.3
  235.5 63.2 all-gather.7
  328.2 48.9 all-gather.5
